TPU v7x, 32 devices: a whole 2x2x4 slice. The times are simulated.
32 devices in a mesh: energy: 8 (over z, y), space: 4 (over x, core).
Axes of the slice: x: 2, y: 2, z: 4, core: 2. Of those that a mesh axis runs over, the one named last changes fastest.
Arguments:
- lesser: bfloat16 [2, 512, 4, 65536], P(None, 'energy', 'space'), may hold values from -6 to 6
- greater: bfloat16 [2, 512, 4, 65536], P(None, 'energy', 'space'), may hold values from -6 to 6
- vdiag: bfloat16 [4, 256, 256], P('space'), may hold values from -0.375 to 0.375
- vlower: bfloat16 [4, 256, 256], P('space'), may hold values from -0.375 to 0.375
- occupancy: int32 [4, 8], P('space'), may hold values from 1 to 32, 128 in all within a row
- tile_order: int32 [4, 512], P('space'), may hold values from 0 to 511, each once within a row
Outputs:
- interaction_diag: bfloat16 [2, 512, 4, 256, 256], P(None, 'energy', 'space')
- interaction_lower: bfloat16 [2, 512, 4, 256, 256], P(None, 'energy', 'space')
Inputs may be any that keep to these rules, and one draw needn't show every extreme that they name: `occupancy`: for each block, the entries sum to 128 and the largest is exactly 32. `tile_order`: each row is a permutation of the tile numbers.
All inputs are finite; a program needn't handle non-finite values.
Results may differ from a plain program's by a relative error of at most 0.015.
Values may be sent and summed in bfloat16 or wider, within the bound.
A program may use at most 448 MiB of HBM per device.

v0:
```python
import jax
import jax.numpy as jnp
from jax import lax
from jax.sharding import PartitionSpec as P

TILE = 128
NNZ = 128


def passed_along(value, axis, steps):
    count = lax.axis_size(axis)
    leading, last = (max(0, -steps), min(count, count - steps))
    return lax.ppermute(value, axis, [(source, source + steps) for source in range(leading, last)])


def split_table(table):
    upper = table.astype(jnp.bfloat16)
    rest = (table - upper.astype(jnp.float32)).astype(jnp.bfloat16)
    return (upper, rest)


def table_times(parts, data):
    first = jnp.dot(parts[0], data, preferred_element_type=jnp.float32)
    return first + jnp.dot(parts[1], data, preferred_element_type=jnp.float32)


def split_times(parts, data):
    upper, rest = split_table(data)
    total = jnp.dot(parts[0], upper, preferred_element_type=jnp.float32)
    total = total + jnp.dot(parts[0], rest, preferred_element_type=jnp.float32)
    return total + jnp.dot(parts[1], upper, preferred_element_type=jnp.float32)


def unpack_tiles(tiles, index, local_energies, n_tiles, width):
    field = jnp.zeros((2, local_energies, n_tiles + 1, tiles.shape[-1]), jnp.bfloat16)
    field = field.at[:, :, index, :].set(tiles)
    return field[:, :, :n_tiles, :].reshape(2, local_energies, width, width)


def per_device(lesser, greater, vdiag, vlower, occupancy, tile_order):
    group_size = lax.axis_size("energy")
    local_energies = lesser.shape[1]
    width = vdiag.shape[1]
    n_tiles = lesser.shape[3] // TILE
    most_tiles = 2 * NNZ // group_size
    counts = occupancy[0]
    tile_perm = tile_order[0]
    slot_ids = jnp.arange(most_tiles, dtype=jnp.int32)
    flat_slot = jnp.arange(group_size, dtype=jnp.int32)[:, None] * most_tiles + slot_ids[None, :]
    listing = jnp.where(slot_ids[None, :] < counts[:, None], tile_perm[flat_slot], n_tiles)
    slot_index = listing.reshape(-1)

    def pack(source):
        tiled = source.reshape(2, local_energies, n_tiles, TILE)
        padded = jnp.concatenate(
            [tiled, jnp.zeros((2, local_energies, 1, TILE), source.dtype)], axis=2
        )
        taken = jnp.take(padded, slot_index, axis=2)
        return taken.reshape(2, local_energies, group_size, most_tiles, TILE)

    lesser_got, greater_got = (
        lax.all_to_all(pack(lesser), "energy", split_axis=2, concat_axis=1, tiled=True),
        lax.all_to_all(pack(greater), "energy", split_axis=2, concat_axis=1, tiled=True),
    )
    energies = local_energies * group_size
    columns = most_tiles * TILE
    lesser_cols = lesser_got.reshape(2, energies, columns)
    greater_cols = greater_got.reshape(2, energies, columns)
    grid = jnp.arange(energies, dtype=jnp.int32)
    phase = (grid[:, None] * grid[None, :] % energies).astype(jnp.float32) * (
        2.0 * jnp.pi / energies
    )
    cos_parts = split_table(jnp.cos(phase))
    sin_parts = split_table(jnp.sin(phase))
    first_real = table_times(cos_parts, lesser_cols[0]) + table_times(sin_parts, lesser_cols[1])
    first_imag = table_times(cos_parts, lesser_cols[1]) - table_times(sin_parts, lesser_cols[0])
    second_real = table_times(cos_parts, greater_cols[0]) - table_times(sin_parts, greater_cols[1])
    second_imag = table_times(cos_parts, greater_cols[1]) + table_times(sin_parts, greater_cols[0])
    product_real = first_real * second_real - first_imag * second_imag
    product_imag = first_real * second_imag + first_imag * second_real
    stacked = jnp.concatenate([product_real, product_imag], axis=1)
    cos_side = split_times(cos_parts, stacked)
    sin_side = split_times(sin_parts, stacked)
    factor = float(energies) ** (-1.5)
    polar_real = factor * (cos_side[:, :columns] - sin_side[:, columns:])
    polar_imag = factor * (cos_side[:, columns:] + sin_side[:, :columns])
    polar_tiles = jnp.stack([polar_real, polar_imag]).astype(jnp.bfloat16)
    polar_tiles = polar_tiles.reshape(2, group_size, local_energies, 1, most_tiles, TILE)
    returned = lax.all_to_all(polar_tiles, "energy", split_axis=1, concat_axis=3, tiled=True)
    returned = returned.reshape(2, local_energies, group_size * most_tiles, TILE)
    own_block = unpack_tiles(returned, slot_index, local_energies, n_tiles, width)
    diag_here = vdiag[0]
    lower_here = vlower[0]
    below_polar, below_diag = passed_along((own_block, diag_here), "space", 1)
    above_polar, above_lower = passed_along((own_block, lower_here), "space", -1)
    left_prod = jnp.einsum(
        "ab,xebc->xeac", lower_here, below_polar, preferred_element_type=jnp.float32
    ).astype(jnp.bfloat16)
    middle_prod = jnp.einsum(
        "ab,xebc->xeac", diag_here, own_block, preferred_element_type=jnp.float32
    ).astype(jnp.bfloat16)
    right_prod = jnp.einsum(
        "ba,xebc->xeac", above_lower, above_polar, preferred_element_type=jnp.float32
    ).astype(jnp.bfloat16)
    diag_sum = jnp.einsum(
        "xeab,cb->xeac", left_prod, lower_here, preferred_element_type=jnp.float32
    )
    diag_sum = diag_sum + jnp.einsum(
        "xeab,bc->xeac", middle_prod, diag_here, preferred_element_type=jnp.float32
    )
    diag_sum = diag_sum + jnp.einsum(
        "xeab,bc->xeac", right_prod, above_lower, preferred_element_type=jnp.float32
    )
    lower_sum = jnp.einsum(
        "xeab,bc->xeac", left_prod, below_diag, preferred_element_type=jnp.float32
    )
    lower_sum = lower_sum + jnp.einsum(
        "xeab,cb->xeac", middle_prod, lower_here, preferred_element_type=jnp.float32
    )
    diag_out = diag_sum.astype(jnp.bfloat16).reshape(2, local_energies, 1, width, width)
    lower_out = lower_sum.astype(jnp.bfloat16).reshape(2, local_energies, 1, width, width)
    return (diag_out, lower_out)


def solution(mesh):
    return jax.shard_map(
        per_device,
        mesh=mesh,
        in_specs=(
            P(None, "energy", "space", None),
            P(None, "energy", "space", None),
            P("space", None, None),
            P("space", None, None),
            P("space", None),
            P("space", None),
        ),
        out_specs=(P(None, "energy", "space", None, None), P(None, "energy", "space", None, None)),
        check_vma=False,
    )
```

profile of v0, /device:TPU:1, one launch (start us, length us, event | category | flops | bytes accessed | tf_op | source)
XLA Modules:
  0.0 1499.1 jit_solution(4860167797015654437)
XLA Ops:
  4.2 9.7 copy.89
  13.9 37.2 %copy.60 = bf16[2,64,512,128]{3,1,2,0:T(8,128)(2,1)S(1)} copy(bf16[2,64,512,128]{3,2,1,0:T(8,128)(2,1)S(1)} %bitcast.170) | data formatting | bytes 33554432 | tf_op jit(solution)/shard_map/reshape | solution.py:54
  51.1 9.7 copy.92
  60.8 40.3 %copy.62 = bf16[2,64,512,128]{3,1,2,0:T(8,128)(2,1)} copy(bf16[2,64,512,128]{3,2,1,0:T(8,128)(2,1)S(1)} %bitcast.171) | data formatting | bytes 33554432 | tf_op jit(solution)/shard_map/reshape | solution.py:54
  101.1 9.1 concatenate.17
  112.6 8.5 concatenate.18
  121.1 14.4 gather_fusion.1
  135.5 14.9 gather_fusion.2
  150.4 11.9 broadcast_select_fusion
  162.3 13.7 copy.63
  176.0 6.6 all-to-all-start.1
  182.6 13.8 copy.61
  196.4 168.3 %all-to-all-done.1 = bf16[2,64,8,32,128]{4,3,1,0,2:T(8,128)(2,1)} async-done(((bf16[2,64,8,32,128]{4,3,1,0,2:T(8,128)(2,1)}), bf16[2,64,8,32,128]{4,3,1,0,2:T(8,128)(2,1)}, u32[]{:S(2)}, u32[]{:S(2)}) %all-to-all-start.1) | async-done | bytes 8388640 | tf_op jit(solution)/shard_map/all_to_all | solution.py:63
  364.7 5.2 all-to-all-start
  370.0 5.6 fusion.197
  375.5 8.9 fusion.36
  384.4 8.9 fusion.34
  393.3 157.9 %all-to-all-done = bf16[2,64,8,32,128]{4,3,1,0,2:T(8,128)(2,1)} async-done(((bf16[2,64,8,32,128]{4,3,1,0,2:T(8,128)(2,1)}), bf16[2,64,8,32,128]{4,3,1,0,2:T(8,128)(2,1)}, u32[]{:S(2)}, u32[]{:S(2)}) %all-to-all-start) | async-done | bytes 8388640 | tf_op jit(solution)/shard_map/all_to_all | solution.py:62
  551.2 4.2 fusion.198
  555.4 9.3 fusion.48
  564.8 8.9 fusion.50
  573.7 9.1 fusion.29
  582.7 9.2 fusion.24
  592.0 9.0 fusion.26
  601.0 9.0 fusion.32
  610.0 9.1 fusion.43
  619.1 8.9 fusion.38
  628.0 8.9 fusion.40
  636.9 9.3 fusion.46
  646.3 15.4 %add_subtract_fusion.1 = f32[512,4096]{1,0:T(8,128)S(1)} fusion(f32[512,4096]{1,0:T(8,128)} %fusion.29, f32[512,4096]{1,0:T(8,128)} %fusion.36, f32[512,4096]{1,0:T(8,128)} %fusion.34, bf16[64,8,32,128]{3,2,1,0:T(8,128)(2,1)} %bitcast.185), kind=kOutput, calls=%fused_computation.36 | convolution fusion | flops 2158493696 | bytes 37748736 | tf_op jit(solution)/shard_map/dot_general | solution.py:24
  661.7 18.6 %add_add_fusion.3 = f32[512,4096]{1,0:T(8,128)} fusion(f32[512,4096]{1,0:T(8,128)} %fusion.43, f32[512,4096]{1,0:T(8,128)} %fusion.50, f32[512,4096]{1,0:T(8,128)} %fusion.48, bf16[64,8,32,128]{3,2,1,0:T(8,128)(2,1)} %bitcast.192), kind=kOutput, calls=%fused_computation.37 | convolution fusion | flops 2158493696 | bytes 37748736 | tf_op jit(solution)/shard_map/dot_general | solution.py:24
  680.3 15.8 %add_add_fusion.2 = f32[512,4096]{1,0:T(8,128)} fusion(f32[512,4096]{1,0:T(8,128)} %fusion.32, f32[512,4096]{1,0:T(8,128)} %fusion.26, f32[512,4096]{1,0:T(8,128)} %fusion.24, bf16[64,8,32,128]{3,2,1,0:T(8,128)(2,1)S(1)} %bitcast.180), kind=kOutput, calls=%fused_computation.34 | convolution fusion | flops 2158493696 | bytes 37748736 | tf_op jit(solution)/shard_map/dot_general | solution.py:24
  696.1 25.4 %multiply_subtract_fusion = (f32[512,4096]{1,0:T(8,128)}, f32[512,4096]{1,0:T(8,128)}) fusion(f32[512,4096]{1,0:T(8,128)} %add_add_fusion.2, f32[512,4096]{1,0:T(8,128)} %add_add_fusion.3, f32[512,4096]{1,0:T(8,128)S(1)} %add_subtract_fusion.1, f32[512,4096]{1,0:T(8,128)} %fusion.46, bf16[64,8,32,128]{3,2,1,0:T(8,128)(2,1)} %bitcast.184, ...), kind=kOutput, calls=%fused_computation.33 | convolution fusion | flops 2171076608 | bytes 71303168 | tf_op jit(solution)/shard_map/dot_general | solution.py:24
  721.5 19.7 %fusion.77 = f32[512,8192]{1,0:T(8,128)} fusion(f32[512,4096]{1,0:T(8,128)} %get-tuple-element.16, f32[512,4096]{1,0:T(8,128)} %get-tuple-element.15), kind=kOutput, calls=%fused_computation.100 | convolution fusion | flops 4319870976 | bytes 33554432 | tf_op jit(solution)/shard_map/dot_general | solution.py:30
  741.2 20.0 %fusion.79 = f32[512,8192]{1,0:T(8,128)} fusion(f32[512,4096]{1,0:T(8,128)} %get-tuple-element.16, f32[512,4096]{1,0:T(8,128)} %get-tuple-element.15), kind=kOutput, calls=%fused_computation.101 | convolution fusion | flops 4315676672 | bytes 33554432 | tf_op jit(solution)/shard_map/dot_general | solution.py:29
  761.2 20.1 %fusion.86 = f32[512,8192]{1,0:T(8,128)} fusion(f32[512,4096]{1,0:T(8,128)} %get-tuple-element.16, f32[512,4096]{1,0:T(8,128)} %get-tuple-element.15), kind=kOutput, calls=%fused_computation.103 | convolution fusion | flops 4319870976 | bytes 33554432 | tf_op jit(solution)/shard_map/dot_general | solution.py:30
  781.4 20.2 %fusion.88 = f32[512,8192]{1,0:T(8,128)} fusion(f32[512,4096]{1,0:T(8,128)} %get-tuple-element.16, f32[512,4096]{1,0:T(8,128)} %get-tuple-element.15), kind=kOutput, calls=%fused_computation.104 | convolution fusion | flops 4315676672 | bytes 33554432 | tf_op jit(solution)/shard_map/dot_general | solution.py:29
  801.6 23.7 %add_add_fusion.1 = f32[512,8192]{1,0:T(8,128)} fusion(f32[512,8192]{1,0:T(8,128)} %fusion.79, f32[512,8192]{1,0:T(8,128)} %fusion.77, f32[512,4096]{1,0:T(8,128)} %get-tuple-element.16, f32[512,4096]{1,0:T(8,128)} %get-tuple-element.15), kind=kOutput, calls=%fused_computation.17 | convolution fusion | flops 4324851712 | bytes 67108864 | tf_op jit(solution)/shard_map/dot_general | solution.py:31
  825.3 23.7 %add_add_fusion = f32[512,8192]{1,0:T(8,128)} fusion(f32[512,8192]{1,0:T(8,128)} %fusion.88, f32[512,8192]{1,0:T(8,128)} %fusion.86, f32[512,4096]{1,0:T(8,128)} %get-tuple-element.16, f32[512,4096]{1,0:T(8,128)} %get-tuple-element.15), kind=kOutput, calls=%fused_computation.16 | convolution fusion | flops 4324851712 | bytes 67108864 | tf_op jit(solution)/shard_map/dot_general | solution.py:31
  849.1 12.9 fusion.22
  862.0 3.3 copy.95
  865.3 3.3 copy.96
  868.6 6.3 pad_maximum_fusion.1
  875.0 5.7 all-to-all-start.2
  880.8 181.1 %all-to-all-done.2 = bf16[2,8,64,1,32,128]{5,4,2,3,0,1:T(8,128)(2,1)} async-done(((bf16[2,8,64,1,32,128]{5,4,2,3,0,1:T(8,128)(2,1)}), bf16[2,8,64,1,32,128]{5,4,2,3,0,1:T(8,128)(2,1)}, u32[]{:S(2)}, u32[]{:S(2)}) %all-to-all-start.2) | async-done | bytes 8388640 | tf_op jit(solution)/shard_map/all_to_all | solution.py:89
  1061.9 9.4 copy.66
  1071.3 12.2 copy.67
  1083.5 6.1 broadcast_in_dim.13
  1089.5 41.1 %scatter_fusion = bf16[2,64,513,128]{3,1,2,0:T(8,128)(2,1)} fusion(bf16[2,64,513,128]{3,1,2,0:T(8,128)(2,1)} %broadcast_in_dim.13, s32[256]{0:T(256)S(1)} %bitcast.197, bf16[256,2,64,128]{3,2,1,0:T(8,128)(2,1)} %copy.67), kind=kCustom, calls=%fused_computation.3 | custom fusion | bytes 25166848 | tf_op jit(solution)/shard_map/scatter | solution.py:36
  1130.6 8.1 slice.58
  1138.7 36.2 %copy.68 = bf16[2,64,512,128]{3,2,1,0:T(8,128)(2,1)} copy(bf16[2,64,512,128]{3,1,2,0:T(8,128)(2,1)S(1)} %slice.58) | data formatting | bytes 33554432 | tf_op jit(solution)/shard_map/slice | solution.py:37
  1174.9 24.4 %reshape.176 = bf16[2,64,256,256]{3,2,1,0:T(8,128)(2,1)} reshape(bf16[2,64,512,128]{3,2,1,0:T(8,128)(2,1)} %copy.68) | data formatting | bytes 33554432 | tf_op jit(solution)/shard_map/reshape | solution.py:37
  1199.3 21.2 %copy.69 = bf16[2,64,256,256]{2,3,1,0:T(8,128)(2,1)} copy(bf16[2,64,256,256]{3,2,1,0:T(8,128)(2,1)} %reshape.176) | data formatting | bytes 33554432 | tf_op jit(solution)/shard_map/reshape | solution.py:37
  1220.6 6.1 collective-permute-start
  1226.7 6.0 collective-permute-start.1
  1234.6 2.4 collective-permute-start.2
  1237.0 12.1 convolution_convert_fusion
  1249.1 21.4 %fusion.1 = f32[2,64,256,256]{3,2,1,0:T(8,128)} fusion(bf16[2,64,256,256]{3,2,1,0:T(8,128)(2,1)} %convolution_convert_fusion, bf16[1,256,256]{2,1,0:T(8,128)(2,1)S(1)} %copy-done.9), kind=kOutput, calls=%fused_computation.8 | convolution fusion | flops 4294967296 | bytes 50462720 | tf_op jit(solution)/shard_map/xeab,cb->xeac/dot_general | solution.py:117
  1270.6 21.4 %fusion.3 = f32[2,64,256,256]{3,2,1,0:T(8,128)} fusion(bf16[2,64,256,256]{3,2,1,0:T(8,128)(2,1)} %convolution_convert_fusion, bf16[1,256,256]{2,1,0:T(8,128)(2,1)S(1)} %copy-done.10), kind=kOutput, calls=%fused_computation.10 | convolution fusion | flops 4294967296 | bytes 50462720 | tf_op jit(solution)/shard_map/xeab,bc->xeac/dot_general | solution.py:108
  1292.0 115.2 %collective-permute-done = bf16[2,64,256,256]{2,3,1,0:T(8,128)(2,1)} collective-permute-done((bf16[2,64,256,256]{2,3,1,0:T(8,128)(2,1)}, bf16[2,64,256,256]{2,3,1,0:T(8,128)(2,1)}, u32[]{:S(2)}, u32[]{:S(2)}) %collective-permute-start) | collective-permute-done | bytes 16777248 | tf_op jit(solution)/shard_map/ppermute | solution.py:13
  1407.2 12.1 convolution_convert_fusion.1
  1419.4 21.4 %fusion.6 = f32[2,64,256,256]{3,2,1,0:T(8,128)} fusion(bf16[2,64,256,256]{3,2,1,0:T(8,128)(2,1)} %convolution_convert_fusion.1, bf16[1,256,256]{2,1,0:T(8,128)(2,1)S(1)} %copy-done.9), kind=kOutput, calls=%fused_computation.13 | convolution fusion | flops 4294967296 | bytes 50462720 | tf_op jit(solution)/shard_map/xeab,cb->xeac/dot_general | solution.py:105
  1440.8 23.6 %fusion.12 = bf16[2,64,1,256,256]{4,3,2,1,0:T(8,128)(2,1)} fusion(f32[2,64,256,256]{3,2,1,0:T(8,128)} %fusion.1, bf16[2,64,256,256]{3,2,1,0:T(8,128)(2,1)} %convolution_convert_fusion.1, bf16[256,256]{1,0:T(8,128)(2,1)S(1)} %collective-permute-done.3), kind=kOutput, calls=%fused_computation.23 | convolution fusion | flops 4311744512 | bytes 67239936 | tf_op jit(solution)/shard_map/xeab,bc->xeac/dot_general | solution.py:114
  1464.4 34.4 %fusion.15 = bf16[2,64,1,256,256]{4,3,2,1,0:T(8,128)(2,1)} fusion(bf16[2,64,256,256]{2,3,1,0:T(8,128)(2,1)} %collective-permute-done.1, f32[2,64,256,256]{3,2,1,0:T(8,128)} %fusion.6, f32[2,64,256,256]{3,2,1,0:T(8,128)} %fusion.3, bf16[256,256]{1,0:T(8,128)(2,1)S(1)} %collective-permute-done.2), kind=kOutput, calls=%fused_computation.24 | convolution fusion | flops 8623489024 | bytes 100794368 | tf_op jit(solution)/shard_map/xeab,bc->xeac/dot_general | solution.py:111
  (43 shorter events, 8.0 us)
Async XLA Ops:
  0.6 0.7 copy-start
  4.1 9.8 copy-start.11
  101.1 11.5 copy-start.2
  176.0 188.8 %all-to-all-start.1 = ((bf16[2,64,8,32,128]{4,3,1,0,2:T(8,128)(2,1)}), bf16[2,64,8,32,128]{4,3,1,0,2:T(8,128)(2,1)}, u32[]{:S(2)}, u32[]{:S(2)}) async-start(bf16[2,64,8,32,128]{4,3,1,0,2:T(8,128)(2,1)} %copy.63), calls=%async_computation.1 | async-start | bytes 16777216 | tf_op jit(solution)/shard_map/all_to_all | solution.py:63
  364.7 186.4 %all-to-all-start = ((bf16[2,64,8,32,128]{4,3,1,0,2:T(8,128)(2,1)}), bf16[2,64,8,32,128]{4,3,1,0,2:T(8,128)(2,1)}, u32[]{:S(2)}, u32[]{:S(2)}) async-start(bf16[2,64,8,32,128]{4,3,1,0,2:T(8,128)(2,1)} %copy.61), calls=%async_computation | async-start | bytes 16777216 | tf_op jit(solution)/shard_map/all_to_all | solution.py:62
  375.5 8.9 copy-start.3
  555.4 72.6 %copy-start.7 = (bf16[1,8,64,1,32,128]{5,4,2,0,1,3:T(8,128)(2,1)}, bf16[1,8,64,1,32,128]{5,4,2,0,1,3:T(8,128)(2,1)S(1)}, u32[]{:S(2)}) copy-start(bf16[1,8,64,1,32,128]{5,4,2,0,1,3:T(8,128)(2,1)S(1)} %get-tuple-element.19) | copy-start | bytes 12582916
  555.4 81.5 %copy-start.5 = (bf16[1,8,64,1,32,128]{5,4,2,0,1,3:T(8,128)(2,1)}, bf16[1,8,64,1,32,128]{5,4,2,0,1,3:T(8,128)(2,1)S(1)}, u32[]{:S(2)}) copy-start(bf16[1,8,64,1,32,128]{5,4,2,0,1,3:T(8,128)(2,1)S(1)} %get-tuple-element.20) | copy-start | bytes 12582916
  564.8 8.9 copy-start.6
  592.0 9.0 copy-start.4
  865.3 3.3 copy-start.8
  875.0 5.7 copy-start.12
  875.0 186.9 %all-to-all-start.2 = ((bf16[2,8,64,1,32,128]{5,4,2,3,0,1:T(8,128)(2,1)}), bf16[2,8,64,1,32,128]{5,4,2,3,0,1:T(8,128)(2,1)}, u32[]{:S(2)}, u32[]{:S(2)}) async-start(bf16[2,8,64,1,32,128]{5,4,2,3,0,1:T(8,128)(2,1)} %pad_maximum_fusion.1), calls=%async_computation.2 | async-start | bytes 16777216 | tf_op jit(solution)/shard_map/all_to_all | solution.py:89
  1199.3 33.3 %copy-start.10 = (bf16[1,256,256]{2,1,0:T(8,128)(2,1)S(1)}, bf16[1,256,256]{2,1,0:T(8,128)(2,1)}, u32[]{:S(2)}) copy-start(bf16[1,256,256]{2,1,0:T(8,128)(2,1)} %param.10) | copy-start | bytes 393220
  1199.3 35.3 %copy-start.9 = (bf16[1,256,256]{2,1,0:T(8,128)(2,1)S(1)}, bf16[1,256,256]{2,1,0:T(8,128)(2,1)}, u32[]{:S(2)}) copy-start(bf16[1,256,256]{2,1,0:T(8,128)(2,1)} %param.11) | copy-start | bytes 393220
  1220.6 186.7 %collective-permute-start = (bf16[2,64,256,256]{2,3,1,0:T(8,128)(2,1)}, bf16[2,64,256,256]{2,3,1,0:T(8,128)(2,1)}, u32[]{:S(2)}, u32[]{:S(2)}) collective-permute-start(bf16[2,64,256,256]{2,3,1,0:T(8,128)(2,1)} %copy.69), channel_id=1, source_target_pairs={{0,1},{1,2},{2,3},{4,5},{5,6},{6,7},{8,9},{9,10},{10,11},{12,13},{... | collective-permute-start | bytes 50331656 | tf_op jit(solution)/shard_map/ppermute | solution.py:13
  1226.7 237.8 %collective-permute-start.1 = (bf16[2,64,256,256]{2,3,1,0:T(8,128)(2,1)}, bf16[2,64,256,256]{2,3,1,0:T(8,128)(2,1)}, u32[]{:S(2)}, u32[]{:S(2)}) collective-permute-start(bf16[2,64,256,256]{2,3,1,0:T(8,128)(2,1)} %copy.69), channel_id=1, source_target_pairs={{1,0},{2,1},{3,2},{5,4},{6,5},{7,6},{9,8},{10,9},{11,10},{13,12},{... | collective-permute-start | bytes 50331656 | tf_op jit(solution)/shard_map/ppermute | solution.py:13
  1232.7 208.1 %collective-permute-start.3 = (bf16[256,256]{1,0:T(8,128)(2,1)S(1)}, bf16[256,256]{1,0:T(8,128)(2,1)S(1)}, u32[]{:S(2)}, u32[]{:S(2)}) collective-permute-start(bf16[256,256]{1,0:T(8,128)(2,1)S(1)} %bitcast.196), channel_id=1, source_target_pairs={{0,1},{1,2},{2,3},{4,5},{5,6},{6,7},{8,9},{9,10},{10,11},{12,13},{... | collective-permute-start | bytes 393224 | tf_op jit(solution)/shard_map/ppermute | solution.py:13
  1234.6 229.8 %collective-permute-start.2 = (bf16[256,256]{1,0:T(8,128)(2,1)S(1)}, bf16[256,256]{1,0:T(8,128)(2,1)S(1)}, u32[]{:S(2)}, u32[]{:S(2)}) collective-permute-start(bf16[256,256]{1,0:T(8,128)(2,1)S(1)} %bitcast.195), channel_id=1, source_target_pairs={{1,0},{2,1},{3,2},{5,4},{6,5},{7,6},{9,8},{10,9},{11,10},{13,12},{... | collective-permute-start | bytes 393224 | tf_op jit(solution)/shard_map/ppermute | solution.py:13
  1464.4 34.5 %copy-start.1 = (s32[1,512]{1,0:T(1,128)S(1)}, s32[1,512]{1,0:T(1,128)}, u32[]{:S(2)}) copy-start(s32[1,512]{1,0:T(1,128)} %param.13) | copy-start | bytes 6148
where the time goes:
time: 1510 us; the launch traced here: 1500 us
  waiting for transfers between devices  623 us (41%)
  matrix products  458 us (30%)
  local copies, waits for them, and re-layouts  352 us (23%)
  starting transfers between devices  34 us (2%)
  other arithmetic  32 us (2%)
    all_to_all x1, waiting for transfers between devices, per_device(): lax.all_to_all(polar_tiles, 'energy', split_axis=1, concat_axis=3, tiled=...  181 us
    all_to_all x1, waiting for transfers between devices, per_device(): lax.all_to_all(pack(greater), 'energy', split_axis=2, concat_axis=1, tile...  168 us
    all_to_all x1, waiting for transfers between devices, per_device(): lax.all_to_all(pack(lesser), 'energy', split_axis=2, concat_axis=1, tiled...  158 us
    ppermute x4, waiting for transfers between devices, passed_along(): lax.ppermute(value, axis, [(source, source + steps) for source in range(l...  115 us
    dot_general x8, matrix products, table_times(): return first + jnp.dot(parts[1], data, preferred_element_type=jnp.float32)  112 us
    reshape x2, local copies, waits for them, and re-layouts, pack(): tiled = source.reshape(2, local_energies, n_tiles, TILE)  77.6 us
    dot_general x8, matrix products, table_times(): first = jnp.dot(parts[0], data, preferred_element_type=jnp.float32)  72.3 us
    dot_general x2, matrix products, split_times(): return total + jnp.dot(parts[1], upper, preferred_element_type=jnp.float32)  47.5 us
  transfers between devices with their start and end apart: 7, of which 4 were waited for; matrix products, arithmetic and copies ran while one was open for 10% of the time, Pallas kernels for 0%

commit v1 on v0

--- a/solution.py
+++ b/solution.py
@@ -60,7 +60,12 @@
 
     lesser_got, greater_got = (
         lax.all_to_all(pack(lesser), "energy", split_axis=2, concat_axis=1, tiled=True),
-        lax.all_to_all(pack(greater), "energy", split_axis=2, concat_axis=1, tiled=True),
+        jnp.concatenate(
+            lax.all_to_all(
+                jnp.stack(jnp.split(pack(greater), lax.axis_size("energy"), axis=2)), "energy", 0, 0
+            ),
+            axis=1,
+        ),
     )
     energies = local_energies * group_size
     columns = most_tiles * TILE

time: 1510 us -> 1470 us (0.974)
  waiting for transfers between devices: 623 us -> 588 us
    all_to_all x1, waiting for transfers between devices: 158 us -> 123 us  [per_device(): lax.all_to_all(pack(lesser), 'energy', split_axis=2, concat_axis=1, tiled...]
    unnamed x30 -> x39, local copies, waits for them, and re-layouts: 28.8 us -> 40.4 us
  transfers between devices with their start and end apart: 7 -> 7, of which waited for: 4 -> 4; matrix products, arithmetic and copies ran while one was open for 10% -> 13% of each run, Pallas kernels for 0% -> 0%
where the time goes in v1:
time: 1470 us; the launch traced here: 1460 us
  waiting for transfers between devices  588 us (40%)
  matrix products  456 us (31%)
  local copies, waits for them, and re-layouts  353 us (24%)
  starting transfers between devices  33.7 us (2%)
  other arithmetic  29.5 us (2%)
    all_to_all x1, waiting for transfers between devices, per_device(): lax.all_to_all(polar_tiles, 'energy', split_axis=1, concat_axis=3, tiled=...  181 us
    all_to_all x1, waiting for transfers between devices, per_device(): lax.all_to_all(jnp.stack(jnp.split(pack(greater), lax.axis_size('energy')...  169 us
    all_to_all x1, waiting for transfers between devices, per_device(): lax.all_to_all(pack(lesser), 'energy', split_axis=2, concat_axis=1, tiled...  123 us
    ppermute x4, waiting for transfers between devices, passed_along(): lax.ppermute(value, axis, [(source, source + steps) for source in range(l...  115 us
    dot_general x8, matrix products, table_times(): return first + jnp.dot(parts[1], data, preferred_element_type=jnp.float32)  110 us
    reshape x2, local copies, waits for them, and re-layouts, pack(): tiled = source.reshape(2, local_energies, n_tiles, TILE)  77.6 us
    dot_general x8, matrix products, table_times(): first = jnp.dot(parts[0], data, preferred_element_type=jnp.float32)  71.9 us
    dot_general x2, matrix products, split_times(): return total + jnp.dot(parts[1], upper, preferred_element_type=jnp.float32)  47.4 us
  transfers between devices with their start and end apart: 7, of which 4 were waited for; matrix products, arithmetic and copies ran while one was open for 13% of the time, Pallas kernels for 0%

profile of v1, /device:TPU:1, one launch (start us, length us, event | category | flops | bytes accessed | tf_op | source)
XLA Modules:
  0.0 1461.0 jit_solution(11968208874897855254)
XLA Ops:
  4.2 9.7 copy.124
  13.9 37.2 %copy.80 = bf16[2,64,512,128]{3,1,2,0:T(8,128)(2,1)S(1)} copy(bf16[2,64,512,128]{3,2,1,0:T(8,128)(2,1)S(1)} %bitcast.200) | data formatting | bytes 33554432 | tf_op jit(solution)/shard_map/reshape | solution.py:54
  51.1 9.7 copy.127
  60.8 40.3 %copy.82 = bf16[2,64,512,128]{3,1,2,0:T(8,128)(2,1)} copy(bf16[2,64,512,128]{3,2,1,0:T(8,128)(2,1)S(1)} %bitcast.201) | data formatting | bytes 33554432 | tf_op jit(solution)/shard_map/reshape | solution.py:54
  101.1 9.1 concatenate.17
  112.6 8.5 concatenate.18
  121.1 14.4 gather_fusion.1
  135.5 14.9 %gather_fusion.2 = bf16[256,2,64,128]{3,2,1,0:T(8,128)(2,1)} fusion(bf16[2,64,513,128]{3,1,2,0:T(8,128)(2,1)} %concatenate.18, s32[1024]{0:T(1024)S(1)} %pad_clamp_fusion), kind=kCustom, calls=%fused_computation.1.clone | custom fusion | bytes 16778240 | tf_op jit(solution)/shard_map/jit(_take)/gather | solution.py:58
  150.4 9.6 broadcast_select_fusion
  159.9 3.0 fusion.206
  176.1 6.6 all-to-all-start.1
  182.7 13.6 copy.81
  196.4 168.5 %all-to-all-done.1 = bf16[8,2,64,1,32,128]{5,4,2,3,1,0:T(8,128)(2,1)} async-done(((bf16[8,2,64,1,32,128]{5,4,2,3,1,0:T(8,128)(2,1)}), bf16[8,2,64,1,32,128]{5,4,2,3,1,0:T(8,128)(2,1)}, u32[]{:S(2)}, u32[]{:S(2)}) %all-to-all-start.1) | async-done | bytes 8388640 | tf_op jit(solution)/shard_map/all_to_all | solution.py:64
  364.9 5.2 all-to-all-start
  370.1 4.2 fusion.205
  374.3 9.0 fusion.29
  383.4 8.9 fusion.26
  392.3 8.9 fusion.36
  401.2 9.4 fusion.32
  410.5 8.9 fusion.34
  419.5 8.9 fusion.24
  428.4 122.9 %all-to-all-done = bf16[2,64,8,32,128]{4,3,1,0,2:T(8,128)(2,1)} async-done(((bf16[2,64,8,32,128]{4,3,1,0,2:T(8,128)(2,1)}), bf16[2,64,8,32,128]{4,3,1,0,2:T(8,128)(2,1)}, u32[]{:S(2)}, u32[]{:S(2)}) %all-to-all-start) | async-done | bytes 8388640 | tf_op jit(solution)/shard_map/all_to_all | solution.py:62
  551.3 4.2 fusion.207
  555.6 9.1 fusion.48
  564.7 8.9 fusion.50
  573.5 9.0 fusion.43
  582.5 9.2 fusion.38
  591.7 8.9 fusion.40
  600.5 9.0 fusion.46
  609.5 16.1 %add_subtract_fusion.1 = f32[512,4096]{1,0:T(8,128)S(1)} fusion(f32[512,4096]{1,0:T(8,128)} %fusion.29, f32[512,4096]{1,0:T(8,128)} %fusion.36, f32[512,4096]{1,0:T(8,128)} %fusion.34, bf16[64,8,32,128]{3,2,1,0:T(8,128)(2,1)} %bitcast.214), kind=kOutput, calls=%fused_computation.36 | convolution fusion | flops 2158493696 | bytes 37748736 | tf_op jit(solution)/shard_map/dot_general | solution.py:24
  625.6 15.7 %add_add_fusion.2 = f32[512,4096]{1,0:T(8,128)} fusion(f32[512,4096]{1,0:T(8,128)} %fusion.32, f32[512,4096]{1,0:T(8,128)} %fusion.26, f32[512,4096]{1,0:T(8,128)} %fusion.24, bf16[64,8,32,128]{3,2,1,0:T(8,128)(2,1)S(1)} %bitcast.210), kind=kOutput, calls=%fused_computation.34 | convolution fusion | flops 2158493696 | bytes 37748736 | tf_op jit(solution)/shard_map/dot_general | solution.py:24
  641.3 18.8 %add_add_fusion.3 = f32[512,4096]{1,0:T(8,128)} fusion(f32[512,4096]{1,0:T(8,128)} %fusion.43, f32[512,4096]{1,0:T(8,128)} %fusion.50, f32[512,4096]{1,0:T(8,128)} %fusion.48, bf16[64,8,32,128]{3,2,1,0:T(8,128)(2,1)} %bitcast.222), kind=kOutput, calls=%fused_computation.37 | convolution fusion | flops 2158493696 | bytes 37748736 | tf_op jit(solution)/shard_map/dot_general | solution.py:24
  660.0 23.2 %multiply_subtract_fusion = (f32[512,4096]{1,0:T(8,128)}, f32[512,4096]{1,0:T(8,128)}) fusion(f32[512,4096]{1,0:T(8,128)} %add_add_fusion.2, f32[512,4096]{1,0:T(8,128)} %add_add_fusion.3, f32[512,4096]{1,0:T(8,128)S(1)} %add_subtract_fusion.1, f32[512,4096]{1,0:T(8,128)} %fusion.46, bf16[64,8,32,128]{3,2,1,0:T(8,128)(2,1)S(1)} %bitcast.218, ...), kind=kOutput, calls=%fused_computation.33 | convolution fusion | flops 2171076608 | bytes 71303168 | tf_op jit(solution)/shard_map/dot_general | solution.py:24
  683.3 19.7 %fusion.85 = f32[512,8192]{1,0:T(8,128)} fusion(f32[512,4096]{1,0:T(8,128)} %get-tuple-element.16, f32[512,4096]{1,0:T(8,128)} %get-tuple-element.15), kind=kOutput, calls=%fused_computation.116 | convolution fusion | flops 4319870976 | bytes 33554432 | tf_op jit(solution)/shard_map/dot_general | solution.py:30
  702.9 19.9 %fusion.87 = f32[512,8192]{1,0:T(8,128)} fusion(f32[512,4096]{1,0:T(8,128)} %get-tuple-element.16, f32[512,4096]{1,0:T(8,128)} %get-tuple-element.15), kind=kOutput, calls=%fused_computation.117 | convolution fusion | flops 4315676672 | bytes 33554432 | tf_op jit(solution)/shard_map/dot_general | solution.py:29
  722.8 20.1 %fusion.94 = f32[512,8192]{1,0:T(8,128)} fusion(f32[512,4096]{1,0:T(8,128)} %get-tuple-element.16, f32[512,4096]{1,0:T(8,128)} %get-tuple-element.15), kind=kOutput, calls=%fused_computation.119 | convolution fusion | flops 4319870976 | bytes 33554432 | tf_op jit(solution)/shard_map/dot_general | solution.py:30
  742.9 20.5 %fusion.96 = f32[512,8192]{1,0:T(8,128)} fusion(f32[512,4096]{1,0:T(8,128)} %get-tuple-element.16, f32[512,4096]{1,0:T(8,128)} %get-tuple-element.15), kind=kOutput, calls=%fused_computation.120 | convolution fusion | flops 4315676672 | bytes 33554432 | tf_op jit(solution)/shard_map/dot_general | solution.py:29
  763.4 23.7 %add_add_fusion.1 = f32[512,8192]{1,0:T(8,128)} fusion(f32[512,8192]{1,0:T(8,128)} %fusion.87, f32[512,8192]{1,0:T(8,128)} %fusion.85, f32[512,4096]{1,0:T(8,128)} %get-tuple-element.16, f32[512,4096]{1,0:T(8,128)} %get-tuple-element.15), kind=kOutput, calls=%fused_computation.17 | convolution fusion | flops 4324851712 | bytes 67108864 | tf_op jit(solution)/shard_map/dot_general | solution.py:31
  787.1 23.7 %add_add_fusion = f32[512,8192]{1,0:T(8,128)} fusion(f32[512,8192]{1,0:T(8,128)} %fusion.96, f32[512,8192]{1,0:T(8,128)} %fusion.94, f32[512,4096]{1,0:T(8,128)} %get-tuple-element.16, f32[512,4096]{1,0:T(8,128)} %get-tuple-element.15), kind=kOutput, calls=%fused_computation.16 | convolution fusion | flops 4324851712 | bytes 67108864 | tf_op jit(solution)/shard_map/dot_general | solution.py:31
  810.9 12.7 fusion.22
  823.6 3.3 copy.130
  826.9 3.3 copy.131
  830.2 6.3 pad_maximum_fusion.1
  836.5 5.8 all-to-all-start.2
  842.4 181.1 %all-to-all-done.2 = bf16[2,8,64,1,32,128]{5,4,2,3,0,1:T(8,128)(2,1)} async-done(((bf16[2,8,64,1,32,128]{5,4,2,3,0,1:T(8,128)(2,1)}), bf16[2,8,64,1,32,128]{5,4,2,3,0,1:T(8,128)(2,1)}, u32[]{:S(2)}, u32[]{:S(2)}) %all-to-all-start.2) | async-done | bytes 8388640 | tf_op jit(solution)/shard_map/all_to_all | solution.py:94
  1023.5 9.4 copy.93
  1032.9 12.2 copy.94
  1045.1 6.1 broadcast_in_dim.13
  1051.2 41.3 %scatter_fusion = bf16[2,64,513,128]{3,1,2,0:T(8,128)(2,1)} fusion(bf16[2,64,513,128]{3,1,2,0:T(8,128)(2,1)} %broadcast_in_dim.13, s32[256]{0:T(256)S(1)} %bitcast.227, bf16[256,2,64,128]{3,2,1,0:T(8,128)(2,1)} %copy.94), kind=kCustom, calls=%fused_computation.3 | custom fusion | bytes 25166848 | tf_op jit(solution)/shard_map/scatter | solution.py:36
  1092.5 8.1 slice.58
  1100.7 36.2 %copy.95 = bf16[2,64,512,128]{3,2,1,0:T(8,128)(2,1)} copy(bf16[2,64,512,128]{3,1,2,0:T(8,128)(2,1)S(1)} %slice.58) | data formatting | bytes 33554432 | tf_op jit(solution)/shard_map/slice | solution.py:37
  1136.8 24.4 %reshape.178 = bf16[2,64,256,256]{3,2,1,0:T(8,128)(2,1)} reshape(bf16[2,64,512,128]{3,2,1,0:T(8,128)(2,1)} %copy.95) | data formatting | bytes 33554432 | tf_op jit(solution)/shard_map/reshape | solution.py:37
  1161.3 21.2 %copy.96 = bf16[2,64,256,256]{2,3,1,0:T(8,128)(2,1)} copy(bf16[2,64,256,256]{3,2,1,0:T(8,128)(2,1)} %reshape.178) | data formatting | bytes 33554432 | tf_op jit(solution)/shard_map/reshape | solution.py:37
  1182.5 6.1 collective-permute-start
  1188.6 5.7 collective-permute-start.1
  1196.3 2.4 collective-permute-start.2
  1198.7 12.4 convolution_convert_fusion
  1211.0 21.4 %fusion.1 = f32[2,64,256,256]{3,2,1,0:T(8,128)} fusion(bf16[2,64,256,256]{3,2,1,0:T(8,128)(2,1)} %convolution_convert_fusion, bf16[1,256,256]{2,1,0:T(8,128)(2,1)S(1)} %copy-done.10), kind=kOutput, calls=%fused_computation.8 | convolution fusion | flops 4294967296 | bytes 50462720 | tf_op jit(solution)/shard_map/xeab,cb->xeac/dot_general | solution.py:122
  1232.5 21.4 %fusion.3 = f32[2,64,256,256]{3,2,1,0:T(8,128)} fusion(bf16[2,64,256,256]{3,2,1,0:T(8,128)(2,1)} %convolution_convert_fusion, bf16[1,256,256]{2,1,0:T(8,128)(2,1)S(1)} %copy-done.11), kind=kOutput, calls=%fused_computation.10 | convolution fusion | flops 4294967296 | bytes 50462720 | tf_op jit(solution)/shard_map/xeab,bc->xeac/dot_general | solution.py:113
  1253.9 115.2 %collective-permute-done = bf16[2,64,256,256]{2,3,1,0:T(8,128)(2,1)} collective-permute-done((bf16[2,64,256,256]{2,3,1,0:T(8,128)(2,1)}, bf16[2,64,256,256]{2,3,1,0:T(8,128)(2,1)}, u32[]{:S(2)}, u32[]{:S(2)}) %collective-permute-start) | collective-permute-done | bytes 16777248 | tf_op jit(solution)/shard_map/ppermute | solution.py:13
  1369.1 12.1 convolution_convert_fusion.1
  1381.2 21.4 %fusion.6 = f32[2,64,256,256]{3,2,1,0:T(8,128)} fusion(bf16[2,64,256,256]{3,2,1,0:T(8,128)(2,1)} %convolution_convert_fusion.1, bf16[1,256,256]{2,1,0:T(8,128)(2,1)S(1)} %copy-done.10), kind=kOutput, calls=%fused_computation.13 | convolution fusion | flops 4294967296 | bytes 50462720 | tf_op jit(solution)/shard_map/xeab,cb->xeac/dot_general | solution.py:110
  1402.7 23.6 %fusion.12 = bf16[2,64,1,256,256]{4,3,2,1,0:T(8,128)(2,1)} fusion(f32[2,64,256,256]{3,2,1,0:T(8,128)} %fusion.1, bf16[2,64,256,256]{3,2,1,0:T(8,128)(2,1)} %convolution_convert_fusion.1, bf16[256,256]{1,0:T(8,128)(2,1)S(1)} %collective-permute-done.3), kind=kOutput, calls=%fused_computation.23 | convolution fusion | flops 4311744512 | bytes 67239936 | tf_op jit(solution)/shard_map/xeab,bc->xeac/dot_general | solution.py:119
  1426.3 34.5 %fusion.15 = bf16[2,64,1,256,256]{4,3,2,1,0:T(8,128)(2,1)} fusion(bf16[2,64,256,256]{2,3,1,0:T(8,128)(2,1)} %collective-permute-done.1, f32[2,64,256,256]{3,2,1,0:T(8,128)} %fusion.6, f32[2,64,256,256]{3,2,1,0:T(8,128)} %fusion.3, bf16[256,256]{1,0:T(8,128)(2,1)S(1)} %collective-permute-done.2), kind=kOutput, calls=%fused_computation.24 | convolution fusion | flops 8623489024 | bytes 100794368 | tf_op jit(solution)/shard_map/xeab,bc->xeac/dot_general | solution.py:116
  (53 shorter events, 21.1 us)
Async XLA Ops:
  0.6 0.7 copy-start
  4.1 9.8 copy-start.12
  101.1 11.5 copy-start.2
  176.1 188.8 %all-to-all-start.1 = ((bf16[8,2,64,1,32,128]{5,4,2,3,1,0:T(8,128)(2,1)}), bf16[8,2,64,1,32,128]{5,4,2,3,1,0:T(8,128)(2,1)}, u32[]{:S(2)}, u32[]{:S(2)}) async-start(bf16[8,2,64,1,32,128]{5,4,2,3,1,0:T(8,128)(2,1)} %fusion.71), calls=%async_computation.1 | async-start | bytes 16777216 | tf_op jit(solution)/shard_map/all_to_all | solution.py:64
  364.9 186.4 %all-to-all-start = ((bf16[2,64,8,32,128]{4,3,1,0,2:T(8,128)(2,1)}), bf16[2,64,8,32,128]{4,3,1,0,2:T(8,128)(2,1)}, u32[]{:S(2)}, u32[]{:S(2)}) async-start(bf16[2,64,8,32,128]{4,3,1,0,2:T(8,128)(2,1)} %copy.81), calls=%async_computation | async-start | bytes 16777216 | tf_op jit(solution)/shard_map/all_to_all | solution.py:62
  374.3 36.2 %copy-start.3 = (bf16[1,8,64,1,32,128]{5,4,2,3,0,1:T(8,128)(2,1)}, bf16[1,8,64,1,32,128]{5,4,2,3,0,1:T(8,128)(2,1)S(1)}, u32[]{:S(2)}) copy-start(bf16[1,8,64,1,32,128]{5,4,2,3,0,1:T(8,128)(2,1)S(1)} %get-tuple-element.17) | copy-start | bytes 12582916
  374.3 45.2 %copy-start.5 = (bf16[1,8,64,1,32,128]{5,4,2,3,0,1:T(8,128)(2,1)}, bf16[1,8,64,1,32,128]{5,4,2,3,0,1:T(8,128)(2,1)S(1)}, u32[]{:S(2)}) copy-start(bf16[1,8,64,1,32,128]{5,4,2,3,0,1:T(8,128)(2,1)S(1)} %get-tuple-element.18) | copy-start | bytes 12582916
  555.5 36.2 %copy-start.8 = (bf16[1,8,64,1,32,128]{5,4,2,0,1,3:T(8,128)(2,1)}, bf16[1,8,64,1,32,128]{5,4,2,0,1,3:T(8,128)(2,1)S(1)}, u32[]{:S(2)}) copy-start(bf16[1,8,64,1,32,128]{5,4,2,0,1,3:T(8,128)(2,1)S(1)} %get-tuple-element.27) | copy-start | bytes 12582916
  555.5 45.0 %copy-start.6 = (bf16[1,8,64,1,32,128]{5,4,2,0,1,3:T(8,128)(2,1)}, bf16[1,8,64,1,32,128]{5,4,2,0,1,3:T(8,128)(2,1)S(1)}, u32[]{:S(2)}) copy-start(bf16[1,8,64,1,32,128]{5,4,2,0,1,3:T(8,128)(2,1)S(1)} %get-tuple-element.28) | copy-start | bytes 12582916
  609.5 16.1 %copy-start.4 = (bf16[1,8,64,1,32,128]{5,4,2,3,0,1:T(8,128)(2,1)S(1)}, bf16[1,8,64,1,32,128]{5,4,2,3,0,1:T(8,128)(2,1)}, u32[]{:S(2)}) copy-start(bf16[1,8,64,1,32,128]{5,4,2,3,0,1:T(8,128)(2,1)} %copy-done.3) | copy-start | bytes 12582916
  641.3 18.8 %copy-start.7 = (bf16[1,8,64,1,32,128]{5,4,2,0,1,3:T(8,128)(2,1)S(1)}, bf16[1,8,64,1,32,128]{5,4,2,0,1,3:T(8,128)(2,1)}, u32[]{:S(2)}) copy-start(bf16[1,8,64,1,32,128]{5,4,2,0,1,3:T(8,128)(2,1)} %copy-done.6) | copy-start | bytes 12582916
  826.9 3.3 copy-start.9
  836.5 5.8 copy-start.13
  836.5 187.0 %all-to-all-start.2 = ((bf16[2,8,64,1,32,128]{5,4,2,3,0,1:T(8,128)(2,1)}), bf16[2,8,64,1,32,128]{5,4,2,3,0,1:T(8,128)(2,1)}, u32[]{:S(2)}, u32[]{:S(2)}) async-start(bf16[2,8,64,1,32,128]{5,4,2,3,0,1:T(8,128)(2,1)} %pad_maximum_fusion.1), calls=%async_computation.2 | async-start | bytes 16777216 | tf_op jit(solution)/shard_map/all_to_all | solution.py:94
  1161.3 33.1 %copy-start.11 = (bf16[1,256,256]{2,1,0:T(8,128)(2,1)S(1)}, bf16[1,256,256]{2,1,0:T(8,128)(2,1)}, u32[]{:S(2)}) copy-start(bf16[1,256,256]{2,1,0:T(8,128)(2,1)} %param.10) | copy-start | bytes 393220
  1161.3 35.0 %copy-start.10 = (bf16[1,256,256]{2,1,0:T(8,128)(2,1)S(1)}, bf16[1,256,256]{2,1,0:T(8,128)(2,1)}, u32[]{:S(2)}) copy-start(bf16[1,256,256]{2,1,0:T(8,128)(2,1)} %param.11) | copy-start | bytes 393220
  1182.5 186.7 %collective-permute-start = (bf16[2,64,256,256]{2,3,1,0:T(8,128)(2,1)}, bf16[2,64,256,256]{2,3,1,0:T(8,128)(2,1)}, u32[]{:S(2)}, u32[]{:S(2)}) collective-permute-start(bf16[2,64,256,256]{2,3,1,0:T(8,128)(2,1)} %copy.96), channel_id=1, source_target_pairs={{0,1},{1,2},{2,3},{4,5},{5,6},{6,7},{8,9},{9,10},{10,11},{12,13},{... | collective-permute-start | bytes 50331656 | tf_op jit(solution)/shard_map/ppermute | solution.py:13
  1188.6 237.7 %collective-permute-start.1 = (bf16[2,64,256,256]{2,3,1,0:T(8,128)(2,1)}, bf16[2,64,256,256]{2,3,1,0:T(8,128)(2,1)}, u32[]{:S(2)}, u32[]{:S(2)}) collective-permute-start(bf16[2,64,256,256]{2,3,1,0:T(8,128)(2,1)} %copy.96), channel_id=1, source_target_pairs={{1,0},{2,1},{3,2},{5,4},{6,5},{7,6},{9,8},{10,9},{11,10},{13,12},{... | collective-permute-start | bytes 50331656 | tf_op jit(solution)/shard_map/ppermute | solution.py:13
  1194.3 208.3 %collective-permute-start.3 = (bf16[256,256]{1,0:T(8,128)(2,1)S(1)}, bf16[256,256]{1,0:T(8,128)(2,1)S(1)}, u32[]{:S(2)}, u32[]{:S(2)}) collective-permute-start(bf16[256,256]{1,0:T(8,128)(2,1)S(1)} %bitcast.226), channel_id=1, source_target_pairs={{0,1},{1,2},{2,3},{4,5},{5,6},{6,7},{8,9},{9,10},{10,11},{12,13},{... | collective-permute-start | bytes 393224 | tf_op jit(solution)/shard_map/ppermute | solution.py:13
  1196.3 230.0 %collective-permute-start.2 = (bf16[256,256]{1,0:T(8,128)(2,1)S(1)}, bf16[256,256]{1,0:T(8,128)(2,1)S(1)}, u32[]{:S(2)}, u32[]{:S(2)}) collective-permute-start(bf16[256,256]{1,0:T(8,128)(2,1)S(1)} %bitcast.225), channel_id=1, source_target_pairs={{1,0},{2,1},{3,2},{5,4},{6,5},{7,6},{9,8},{10,9},{11,10},{13,12},{... | collective-permute-start | bytes 393224 | tf_op jit(solution)/shard_map/ppermute | solution.py:13
  1426.3 34.5 %copy-start.1 = (s32[1,512]{1,0:T(1,128)S(1)}, s32[1,512]{1,0:T(1,128)}, u32[]{:S(2)}) copy-start(s32[1,512]{1,0:T(1,128)} %param.13) | copy-start | bytes 6148
